TPU v7x, 32 devices: a whole 2x2x4 slice. The times are simulated.
32 devices in a mesh: row: 4 (over x, core), col: 8 (over z, y).
Axes of the slice: x: 2, y: 2, z: 4, core: 2. Of those that a mesh axis runs over, the one named last changes fastest.
Arguments:
- embeddings: bfloat16 [4096, 512], P(('row', 'col')), may hold values from -6 to 6
- sketch: bfloat16 [4096, 64], P(('row', 'col')), may hold values from -240 to 240
Outputs:
- basis: float32 [4096, 64], P(('row', 'col'))
- first_pass: float32 [4096, 64], P(('row', 'col'))
All inputs are finite; a program needn't handle non-finite values.
Results may differ from a plain program's by a relative error of at most 0.00205.
Values may be sent and summed in bfloat16 or wider, within the bound.
No kernel may reach another device: no remote copies, remote signals or barrier semaphores. Data moves between devices by JAX's collectives and lax.ppermute only.
A program may use at most 64 MiB of HBM per device.

v0:
```python
import jax
import jax.numpy as jnp
from jax import lax
from jax.sharding import PartitionSpec as P


def squares_of(points):
    return jnp.sum(jnp.square(points.astype(jnp.float32)), axis=1)


def kernel_tile(left, right, left_sq, right_sq, gamma):
    cross = lax.dot_general(
        left, right, (((1,), (1,)), ((), ())), preferred_element_type=jnp.float32
    )
    dist = left_sq[:, None] + right_sq[None, :] - 2.0 * cross
    return jnp.exp(-gamma * dist).astype(jnp.bfloat16)


def product_of(left, right):
    return lax.dot_general(
        left,
        right,
        (((0,), (0,)), ((), ())),
        precision=lax.Precision.HIGHEST,
        preferred_element_type=jnp.float32,
    )


def per_device(embeddings, sketch):
    width = embeddings.shape[1]
    gamma = 3.0 / width
    own_points = lax.all_gather(embeddings, "row", axis=0, tiled=True)
    own_sq = squares_of(own_points)
    empty = jnp.zeros((own_points.shape[0], sketch.shape[1]), jnp.float32)
    total = empty
    points = lax.all_gather(embeddings, "col", axis=0, tiled=True)
    tests = lax.all_gather(sketch, "col", axis=0, tiled=True)
    count = points.shape[0]
    size = 512

    def step(carry, block):
        block_points, block_tests = block
        tile = kernel_tile(own_points, block_points, own_sq, squares_of(block_points), gamma)
        return (carry + jnp.dot(tile, block_tests, preferred_element_type=jnp.float32), None)

    stacked = (
        points.reshape(count // size, size, width),
        tests.reshape(count // size, size, tests.shape[1]),
    )
    total, unused = lax.scan(step, total, stacked)
    sketched = lax.psum_scatter(total, "row", scatter_dimension=0, tiled=True)
    core = lax.psum(product_of(sketch.astype(jnp.float32), sketched), ("row", "col"))
    lower = jnp.linalg.cholesky(core)
    first = jax.scipy.linalg.solve_triangular(lower, sketched.T, lower=True).T
    gram_two = lax.psum(product_of(first, first), ("row", "col"))
    lower_two = jnp.linalg.cholesky(gram_two)
    second = jax.scipy.linalg.solve_triangular(lower_two, first.T, lower=True).T
    total_points = sketched.shape[0] * lax.axis_size("row") * lax.axis_size("col")
    scale = jnp.sqrt(jnp.float32(total_points))
    return (second * scale, first * scale)


def solution(mesh):
    placed = (P(("row", "col"), None), P(("row", "col"), None))
    return jax.shard_map(
        per_device,
        mesh=mesh,
        in_specs=placed,
        out_specs=(P(("row", "col"), None), P(("row", "col"), None)),
        check_vma=False,
    )
```

profile of v0, /device:TPU:0, one launch (start us, length us, event | category | flops | bytes accessed | tf_op | source)
XLA Modules:
  0.0 193.4 jit_solution(8559707278417701284)
XLA Ops:
  7.2 0.7 all-gather.2.cloned.1.call-update
  8.0 28.2 %all_gather.11 = bf16[1024,64]{0,1:T(8,128)(2,1)S(1)} all-gather(bf16[128,64]{0,1:T(8,128)(2,1)S(1)} %copy-done.3), channel_id=1, replica_groups=mesh['row'=4,'col'=8] {'col'}, dimensions={0}, use_global_device_ids=true | all-gather | bytes 147456 | tf_op jit(solution)/shard_map/all_gather | solution.py:37
  36.4 0.7 copy-done
  37.1 7.2 %all_gather.9 = bf16[512,512]{1,0:T(8,128)(2,1)S(1)} all-gather(bf16[128,512]{1,0:T(8,128)(2,1)S(1)} %copy-done), channel_id=1, replica_groups=mesh['row'=4,'col'=8] {'row'}, dimensions={0}, use_global_device_ids=true | all-gather | bytes 655360 | tf_op jit(solution)/shard_map/all_gather | solution.py:32
  44.5 9.1 %all-gather.2.cloned.1.call-done = bf16[1024,512]{1,0:T(8,128)(2,1)} async-done(((bf16[128,512]{1,0:T(8,128)(2,1)}), bf16[1024,512]{1,0:T(8,128)(2,1)}) %all-gather.2.cloned.1.call-update) | async-done | bytes 1048592 | tf_op jit(solution)/shard_map/all_gather | solution.py:36
  53.6 6.2 %while.11 = (s32[]{:T(128)}, f32[512,64]{0,1:T(8,128)S(1)}, f32[512]{0:T(512)S(1)}, bf16[2,512,512]{2,1,0:T(8,128)(2,1)}, bf16[512,512]{1,0:T(8,128)(2,1)S(1)}, ...) while((s32[]{:T(128)}, f32[512,64]{0,1:T(8,128)S(1)}, f32[512]{0:T(512)S(1)}, ...), condition=%wide.region_3.4_spmd.clone, body=%wide.region_1.3_spmd.clone.sunk | while | flops 304152064 | bytes 1973347 | solution.py:50
  53.6 1.2 multiply_reduce_fusion.3
  54.8 1.8 fusion.47
  56.6 1.2 multiply_reduce_fusion.3
  57.9 1.8 fusion.47
  59.7 0.6 copy-done.2
  60.4 18.5 %reduce-scatter.2.cloned.1.call-done = f32[128,64]{0,1:T(8,128)} async-done(((f32[512,64]{0,1:T(8,128)}), f32[128,64]{0,1:T(8,128)}) %reduce-scatter.2.cloned.1.call-update) | async-done | bytes 32784 | tf_op jit(solution)/shard_map/reduce_scatter | solution.py:51
  78.9 0.9 convolution_bitcast_fusion
  79.8 39.4 %psum.14 = f32[64,64]{0,1:T(8,128)S(1)} all-reduce(f32[64,64]{0,1:T(8,128)S(1)} %convolution_bitcast_fusion), channel_id=1, replica_groups=mesh['row'=4,'col'=8] {'row','col'}, use_global_device_ids=true, to_apply=%region_5.6 | all-reduce | flops 4096 | bytes 32768 | tf_op jit(solution)/shard_map/psum | solution.py:52
  119.3 5.8 %cholesky.44 = f32[64,64]{1,0:T(8,128)S(1)} custom-call(f32[64,64]{1,0:T(8,128)S(1)} %fusion.30), custom_call_target="Cholesky" | custom-call | tf_op jit(solution)/shard_map/jit(cholesky)/cholesky | solution.py:53
  125.2 0.6 compare_reduce_fusion.1
  125.9 0.7 fusion.23
  126.5 4.9 %custom-call.7 = f32[1,64,64]{1,2,0:T(8,128)S(1)} custom-call(f32[1,64,64]{2,1,0:T(8,128)S(1)} %fusion.23), custom_call_target="InvertDiagBlocksLowerTriangular" | custom-call | tf_op jit(solution)/shard_map/jit(_solve_triangular)/triangular_solve | solution.py:54
  132.5 41.0 %psum.15 = f32[64,64]{0,1:T(8,128)S(1)} all-reduce(f32[64,64]{0,1:T(8,128)S(1)} %fusion.33), channel_id=1, replica_groups=mesh['row'=4,'col'=8] {'row','col'}, use_global_device_ids=true, to_apply=%region_8.11 | all-reduce | flops 4096 | bytes 32768 | tf_op jit(solution)/shard_map/psum | solution.py:55
  173.6 5.8 %cholesky.55 = f32[64,64]{1,0:T(8,128)S(1)} custom-call(f32[64,64]{1,0:T(8,128)S(1)} %fusion.26), custom_call_target="Cholesky" | custom-call | tf_op jit(solution)/shard_map/jit(cholesky)/cholesky | solution.py:56
  179.5 0.6 compare_reduce_fusion
  180.2 0.7 fusion.24
  180.8 4.9 %custom-call.8 = f32[1,64,64]{1,2,0:T(8,128)S(1)} custom-call(f32[1,64,64]{2,1,0:T(8,128)S(1)} %fusion.24), custom_call_target="InvertDiagBlocksLowerTriangular" | custom-call | tf_op jit(solution)/shard_map/jit(_solve_triangular)/triangular_solve | solution.py:57
  185.7 0.9 fusion.22
  (21 shorter events, 1.7 us)
Async XLA Ops:
  7.2 0.8 copy-start.3
  7.2 46.4 %all-gather.2.cloned.1.call-start = ((), (), s32[]{:S(2)}) async-start(), calls=%async_computation.1 | async-start | bytes 1179648 | tf_op jit(solution)/shard_map/all_gather | solution.py:36
  7.9 71.0 %reduce-scatter.2.cloned.1.call-start = ((), (), s32[]{:S(2)}) async-start(), calls=%async_computation.2 | async-start | bytes 163840 | tf_op jit(solution)/shard_map/reduce_scatter | solution.py:51
  36.2 0.9 copy-start
  59.7 0.6 copy-start.2
  125.9 5.6 %copy-start.1 = (f32[128,64]{0,1:T(8,128)S(1)}, f32[128,64]{0,1:T(8,128)}, u32[]{:S(2)}) copy-start(f32[128,64]{0,1:T(8,128)} %reduce-scatter.2.cloned.1.call-done) | copy-start | bytes 98308
Sparse Core Ops, SparseCore 0:
  10.1 43.4 all-gather.1
  60.5 18.3 reduce-scatter.1
where the time goes:
time: 194 us; the launch traced here: 193 us
  blocking collectives  116 us (60%)
  waiting for transfers between devices  28.3 us (15%)
  other arithmetic  27.4 us (14%)
  between operations  14.2 us (7%)
  matrix products  5.88 us (3%)
    psum x1, blocking collectives, per_device(): gram_two = lax.psum(product_of(first, first), ('row', 'col'))  41 us
    psum x1, blocking collectives, per_device(): lax.psum(product_of(sketch.astype(jnp.float32), sketched), ('row', 'col'))  39.4 us
    all_gather x1, blocking collectives, per_device(): tests = lax.all_gather(sketch, 'col', axis=0, tiled=True)  28.2 us
    reduce_scatter x1, waiting for transfers between devices, per_device(): sketched = lax.psum_scatter(total, 'row', scatter_dimension=0, tiled=True)  18.5 us
    all_gather x1, waiting for transfers between devices, per_device(): points = lax.all_gather(embeddings, 'col', axis=0, tiled=True)  9.11 us
    all_gather x1, blocking collectives, per_device(): own_points = lax.all_gather(embeddings, 'row', axis=0, tiled=True)  7.18 us
    another operation x3, other arithmetic, per_device(): lower_two = jnp.linalg.cholesky(gram_two)  6.52 us
    another operation x3, other arithmetic, per_device(): lower = jnp.linalg.cholesky(core)  6.52 us
  transfers between devices with their start and end apart: 2, of which 2 were waited for; matrix products, arithmetic and copies ran while one was open for 0% of the time, Pallas kernels for 0%

commit v1 on v0

--- a/solution.py
+++ b/solution.py
@@ -52,7 +52,9 @@
     core = lax.psum(product_of(sketch.astype(jnp.float32), sketched), ("row", "col"))
     lower = jnp.linalg.cholesky(core)
     first = jax.scipy.linalg.solve_triangular(lower, sketched.T, lower=True).T
-    gram_two = lax.psum(product_of(first, first), ("row", "col"))
+    gram_two = product_of(first, first)
+    for at in ("col", "row"):
+        gram_two = lax.psum(gram_two, at)
     lower_two = jnp.linalg.cholesky(gram_two)
     second = jax.scipy.linalg.solve_triangular(lower_two, first.T, lower=True).T
     total_points = sketched.shape[0] * lax.axis_size("row") * lax.axis_size("col")

time: 194 us -> 200 us (1.031)
  blocking collectives: 116 us -> 122 us
    psum x1 -> x2, blocking collectives: 41 us -> 47.1 us  [per_device(): gram_two = lax.psum(gram_two, at)]
where the time goes in v1:
time: 200 us; the launch traced here: 199 us
  blocking collectives  122 us (61%)
  waiting for transfers between devices  28.3 us (14%)
  other arithmetic  27.4 us (14%)
  between operations  14.2 us (7%)
  matrix products  5.88 us (3%)
    psum x2, blocking collectives, per_device(): gram_two = lax.psum(gram_two, at)  47.1 us
    psum x1, blocking collectives, per_device(): lax.psum(product_of(sketch.astype(jnp.float32), sketched), ('row', 'col'))  39.4 us
    all_gather x1, blocking collectives, per_device(): tests = lax.all_gather(sketch, 'col', axis=0, tiled=True)  28.2 us
    reduce_scatter x1, waiting for transfers between devices, per_device(): sketched = lax.psum_scatter(total, 'row', scatter_dimension=0, tiled=True)  18.5 us
    all_gather x1, waiting for transfers between devices, per_device(): points = lax.all_gather(embeddings, 'col', axis=0, tiled=True)  9.11 us
    all_gather x1, blocking collectives, per_device(): own_points = lax.all_gather(embeddings, 'row', axis=0, tiled=True)  7.18 us
    another operation x3, other arithmetic, per_device(): lower = jnp.linalg.cholesky(core)  6.52 us
    another operation x3, other arithmetic, per_device(): lower_two = jnp.linalg.cholesky(gram_two)  6.52 us
  transfers between devices with their start and end apart: 2, of which 2 were waited for; matrix products, arithmetic and copies ran while one was open for 0% of the time, Pallas kernels for 0%

profile of v1, /device:TPU:0, one launch (start us, length us, event | category | flops | bytes accessed | tf_op | source)
XLA Modules:
  0.0 199.5 jit_solution(7991163948288984322)
XLA Ops:
  7.2 0.7 all-gather.2.cloned.1.call-update
  8.0 28.2 %all_gather.11 = bf16[1024,64]{0,1:T(8,128)(2,1)S(1)} all-gather(bf16[128,64]{0,1:T(8,128)(2,1)S(1)} %copy-done.3), channel_id=1, replica_groups=mesh['row'=4,'col'=8] {'col'}, dimensions={0}, use_global_device_ids=true | all-gather | bytes 147456 | tf_op jit(solution)/shard_map/all_gather | solution.py:37
  36.4 0.7 copy-done
  37.1 7.2 %all_gather.9 = bf16[512,512]{1,0:T(8,128)(2,1)S(1)} all-gather(bf16[128,512]{1,0:T(8,128)(2,1)S(1)} %copy-done), channel_id=1, replica_groups=mesh['row'=4,'col'=8] {'row'}, dimensions={0}, use_global_device_ids=true | all-gather | bytes 655360 | tf_op jit(solution)/shard_map/all_gather | solution.py:32
  44.5 9.1 %all-gather.2.cloned.1.call-done = bf16[1024,512]{1,0:T(8,128)(2,1)} async-done(((bf16[128,512]{1,0:T(8,128)(2,1)}), bf16[1024,512]{1,0:T(8,128)(2,1)}) %all-gather.2.cloned.1.call-update) | async-done | bytes 1048592 | tf_op jit(solution)/shard_map/all_gather | solution.py:36
  53.6 6.2 %while.11 = (s32[]{:T(128)}, f32[512,64]{0,1:T(8,128)S(1)}, f32[512]{0:T(512)S(1)}, bf16[2,512,512]{2,1,0:T(8,128)(2,1)}, bf16[512,512]{1,0:T(8,128)(2,1)S(1)}, ...) while((s32[]{:T(128)}, f32[512,64]{0,1:T(8,128)S(1)}, f32[512]{0:T(512)S(1)}, ...), condition=%wide.region_3.4_spmd.clone, body=%wide.region_1.3_spmd.clone.sunk | while | flops 304152064 | bytes 1973347 | solution.py:50
  53.6 1.2 multiply_reduce_fusion.3
  54.8 1.8 fusion.47
  56.6 1.2 multiply_reduce_fusion.3
  57.9 1.8 fusion.47
  60.4 18.5 %reduce-scatter.2.cloned.1.call-done = f32[128,64]{0,1:T(8,128)} async-done(((f32[512,64]{0,1:T(8,128)}), f32[128,64]{0,1:T(8,128)}) %reduce-scatter.2.cloned.1.call-update) | async-done | bytes 32784 | tf_op jit(solution)/shard_map/reduce_scatter | solution.py:51
  78.9 0.9 convolution_bitcast_fusion
  79.8 39.4 %psum.21 = f32[64,64]{0,1:T(8,128)S(1)} all-reduce(f32[64,64]{0,1:T(8,128)S(1)} %convolution_bitcast_fusion), channel_id=1, replica_groups=mesh['row'=4,'col'=8] {'row','col'}, use_global_device_ids=true, to_apply=%region_5.6 | all-reduce | flops 4096 | bytes 32768 | tf_op jit(solution)/shard_map/psum | solution.py:52
  119.3 5.8 %cholesky.44 = f32[64,64]{1,0:T(8,128)S(1)} custom-call(f32[64,64]{1,0:T(8,128)S(1)} %fusion.30), custom_call_target="Cholesky" | custom-call | tf_op jit(solution)/shard_map/jit(cholesky)/cholesky | solution.py:53
  125.2 0.6 compare_reduce_fusion.1
  125.9 0.7 fusion.23
  126.5 4.9 %custom-call.7 = f32[1,64,64]{1,2,0:T(8,128)S(1)} custom-call(f32[1,64,64]{2,1,0:T(8,128)S(1)} %fusion.23), custom_call_target="InvertDiagBlocksLowerTriangular" | custom-call | tf_op jit(solution)/shard_map/jit(_solve_triangular)/triangular_solve | solution.py:54
  132.5 36.8 %psum.22 = f32[64,64]{0,1:T(8,128)S(1)} all-reduce(f32[64,64]{0,1:T(8,128)S(1)} %fusion.33), channel_id=1, replica_groups=mesh['row'=4,'col'=8] {'col'}, use_global_device_ids=true, to_apply=%region_8.11 | all-reduce | flops 4096 | bytes 32768 | tf_op jit(solution)/shard_map/psum | solution.py:57
  169.3 10.3 %psum.23 = f32[64,64]{0,1:T(8,128)S(1)} all-reduce(f32[64,64]{0,1:T(8,128)S(1)} %psum.22), channel_id=1, replica_groups=mesh['row'=4,'col'=8] {'row'}, use_global_device_ids=true, to_apply=%region_9.12 | all-reduce | flops 4096 | bytes 32768 | tf_op jit(solution)/shard_map/psum | solution.py:57
  179.7 5.8 %cholesky.55 = f32[64,64]{1,0:T(8,128)S(1)} custom-call(f32[64,64]{1,0:T(8,128)S(1)} %fusion.26), custom_call_target="Cholesky" | custom-call | tf_op jit(solution)/shard_map/jit(cholesky)/cholesky | solution.py:58
  185.6 0.6 compare_reduce_fusion
  186.2 0.7 fusion.24
  186.9 4.9 %custom-call.8 = f32[1,64,64]{1,2,0:T(8,128)S(1)} custom-call(f32[1,64,64]{2,1,0:T(8,128)S(1)} %fusion.24), custom_call_target="InvertDiagBlocksLowerTriangular" | custom-call | tf_op jit(solution)/shard_map/jit(_solve_triangular)/triangular_solve | solution.py:59
  191.8 0.9 fusion.22
  (22 shorter events, 2.4 us)
Async XLA Ops:
  7.2 0.8 copy-start.3
  7.2 46.4 %all-gather.2.cloned.1.call-start = ((), (), s32[]{:S(2)}) async-start(), calls=%async_computation.1 | async-start | bytes 1179648 | tf_op jit(solution)/shard_map/all_gather | solution.py:36
  7.9 71.0 %reduce-scatter.2.cloned.1.call-start = ((), (), s32[]{:S(2)}) async-start(), calls=%async_computation.2 | async-start | bytes 163840 | tf_op jit(solution)/shard_map/reduce_scatter | solution.py:51
  36.2 0.9 copy-start
  59.7 0.6 copy-start.2
  125.9 5.6 %copy-start.1 = (f32[128,64]{0,1:T(8,128)S(1)}, f32[128,64]{0,1:T(8,128)}, u32[]{:S(2)}) copy-start(f32[128,64]{0,1:T(8,128)} %reduce-scatter.2.cloned.1.call-done) | copy-start | bytes 98308
Sparse Core Ops, SparseCore 0:
  10.1 43.4 all-gather.1
  60.5 18.3 reduce-scatter.1
